TPU v7x, 256 devices: a whole 4x4x8 slice. The times are simulated.
256 devices in a mesh: subcube: 2 (over y_hi), row: 8 (over z), col: 16 (over x, y_lo, core).
Axes of the slice: x: 4, y: 4 (y_hi: 2, y_lo: 2; y = y_hi * 2 + y_lo), z: 8, core: 2. Of those that a mesh axis runs over, the one named last changes fastest.
Arguments:
- front_entries: float32 [16, 8, 64, 24576], P('col', 'row', None, 'subcube'), may hold values from -6 to 6
- child_blocks: float32 [2, 16, 8, 64, 12288], P('subcube', 'col', 'row'), may hold values from -6 to 6
- row_maps: int32 [2, 12288], replicated, may hold values from 0 to 24575, as said below
- pivot_inverses: float32 [2, 512, 512], P(None, 'row')
- tile_mask: int32 [48, 16], P(('subcube', 'row'), 'col'), may hold values 0 or 1
Outputs:
- factored: float32 [24576, 8192], P(('subcube', 'row'), 'col')
Inputs may be any that keep to these rules, and one draw needn't show every extreme that they name: Each row of row_maps lists 12288 distinct front rows in increasing order; its first is 0 and its last 24575.
All inputs are finite; a program needn't handle non-finite values. No bound on the sum of `tile_mask` on one device may be relied on, other than what follows from the above.
Results may differ from a plain program's by a relative error of at most 0.0001.
Values sent between devices are 32-bit elements; how exact they have to be, the bound alone decides.
No kernel may reach another device: no remote copies, remote signals or barrier semaphores. Data moves between devices by JAX's collectives and lax.ppermute only.
A program may use at most 128 MiB of HBM per device.

v0:
```python
import jax
import jax.numpy as jnp
from jax import lax
from jax.sharding import PartitionSpec as P

PANEL = 512
PANELS = 2


def broadcast(value, axis, source):
    kept = jnp.where(lax.axis_index(axis) == source, value, 0).astype(value.dtype)
    return lax.psum(kept, axis)


def from_partner(x, axis, distance):
    return lax.ppermute(x, axis, [(i, i ^ 1 << distance) for i in range(lax.axis_size(axis))])


def product(left, right):
    return jnp.dot(left, right, precision=lax.Precision.HIGHEST, preferred_element_type=jnp.float32)


def extend_add(target, child_rows, row_map, offset):
    local_rows = row_map - offset
    inside = (local_rows >= 0) & (local_rows < target.shape[1])
    target_rows = jnp.where(inside, local_rows, target.shape[1])
    return target.at[:, target_rows].add(child_rows, mode="drop")


def send_strip(row_strip, root_row):
    return broadcast(row_strip, ("subcube", "row"), root_row)


def local(front_entries, child_blocks, row_maps, pivot_inverses, tile_mask):
    half_rows = front_entries.shape[3]
    subcube_side = lax.axis_index("subcube")
    own_block = child_blocks[0, 0, 0]
    partner_block = from_partner(own_block, "subcube", 0)
    own_map = lax.dynamic_index_in_dim(row_maps, subcube_side, 0, keepdims=False)
    partner_map = lax.dynamic_index_in_dim(row_maps, 1 - subcube_side, 0, keepdims=False)
    assembled = front_entries[0, 0]
    assembled = extend_add(assembled, own_block, own_map, subcube_side * half_rows)
    assembled = extend_add(assembled, partner_block, partner_map, subcube_side * half_rows)
    regrouped = lax.all_to_all(assembled, "row", split_axis=1, concat_axis=0, tiled=True)
    local_block = regrouped.T
    row_count = local_block.shape[0]
    block_width = local_block.shape[1]
    column_place = lax.axis_index("col")
    column_ids = column_place * block_width + jnp.arange(block_width, dtype=jnp.int32)
    grid_row = subcube_side * lax.axis_size("row") + lax.axis_index("row")
    row_ids = grid_row * row_count + jnp.arange(row_count, dtype=jnp.int32)
    kept_tiles = jnp.repeat(jnp.repeat(tile_mask.astype(jnp.float32), PANEL, axis=0), PANEL, axis=1)
    for panel_index in range(PANELS):
        first_col = panel_index * PANEL
        after_col = first_col + PANEL
        owner_col = first_col // block_width
        local_start = first_col - owner_col * block_width
        root_row = first_col // row_count
        row_start = first_col - root_row * row_count
        panel_cols = local_block
        row_strip = local_block[row_start : row_start + PANEL, :]
        inverse = lax.all_gather(pivot_inverses[panel_index], "row", axis=0, tiled=True)
        scaled = broadcast(product(panel_cols, inverse), "col", owner_col)
        across = send_strip(row_strip, root_row)
        update = product(scaled, across)
        below = (row_ids >= after_col).astype(jnp.float32)[:, None]
        live_mask = kept_tiles * (column_ids >= after_col).astype(jnp.float32)[None, :] * below
        local_block = local_block - update * live_mask
        current = local_block
        replace = (column_place == owner_col) & (row_ids >= first_col)[:, None]
        local_block = local_block.at[:, local_start : local_start + PANEL].set(
            jnp.where(replace, scaled, current)
        )
    return local_block


def solution(mesh):
    return jax.shard_map(
        local,
        mesh=mesh,
        in_specs=(
            P("col", "row", None, "subcube"),
            P("subcube", "col", "row", None, None),
            P(),
            P(None, "row", None),
            P(("subcube", "row"), "col"),
        ),
        out_specs=P(("subcube", "row"), "col"),
        check_vma=False,
    )
```

profile of v0, /device:TPU:1, one launch (start us, length us, event | category | flops | bytes accessed | tf_op | source)
XLA Modules:
  0.0 864.5 jit_solution(14957715034153878558)
XLA Ops:
  7.4 3.7 collective-permute-start
  11.1 5.9 copy.10
  17.0 4.0 copy.11
  21.0 0.3 compare_select_fusion
  21.3 64.7 %scatter_fusion = f32[64,12288]{0,1:T(8,128)} fusion(f32[64,12288]{0,1:T(8,128)} %bitcast.31, s32[12288]{0:T(1024)S(1)} %bitcast.39, f32[12288,64]{1,0:T(8,128)} %copy.11), kind=kCustom, calls=%fused_computation | custom fusion | flops 786432 | bytes 9486336 | tf_op jit(solution)/shard_map/scatter-add | solution.py:27
  86.1 5.8 copy.12
  91.8 64.7 %scatter_fusion.1 = f32[64,12288]{0,1:T(8,128)} fusion(f32[64,12288]{0,1:T(8,128)} %scatter_fusion, s32[12288]{0:T(1024)S(1)} %bitcast.38, f32[12288,64]{1,0:T(8,128)} %copy.12), kind=kCustom, calls=%fused_computation.1 | custom fusion | flops 786432 | bytes 9486336 | tf_op jit(solution)/shard_map/scatter-add | solution.py:27
  156.6 6.1 copy.13
  162.7 8.3 all-to-all-start
  171.0 0.7 fusion.17
  171.8 81.7 %all-to-all-done = f32[64,8,1536]{2,0,1:T(8,128)S(1)} async-done(((f32[64,8,1536]{2,0,1:T(8,128)}), f32[64,8,1536]{2,0,1:T(8,128)S(1)}, u32[]{:S(2)}, u32[]{:S(2)}) %all-to-all-start) | async-done | bytes 3145760 | tf_op jit(solution)/shard_map/all_to_all | solution.py:44
  253.6 2.3 copy.14
  255.9 2.4 slice_select_fusion.1
  258.6 12.4 %convolution_select_fusion.1 = f32[1536,512]{1,0:T(8,128)} fusion(f32[512,1536]{1,0:T(8,128)S(1)} %bitcast.34, pred[]{:T(512)S(6)} %eq.13, f32[1,512,512]{2,1,0:T(8,128)} %all-gather.5.cloned.1.call-done), kind=kOutput, calls=%fused_computation.3 | convolution fusion | flops 4832624640 | bytes 7340033 | tf_op jit(solution)/shard_map/dot_general | solution.py:20
  271.0 0.7 all-gather.7.cloned.1.call-update
  271.9 130.9 %all-reduce.7.cloned.1.call-done = f32[512,512]{1,0:T(8,128)} async-done(((f32[512,512]{1,0:T(8,128)}), f32[512,512]{1,0:T(8,128)}) %all-reduce.7.cloned.1.call-update) | async-done | bytes 1048592 | tf_op jit(solution)/shard_map/psum | solution.py:12
  402.8 142.3 %all-reduce.5.cloned.1.call-done = f32[1536,512]{1,0:T(8,128)} async-done(((f32[1536,512]{1,0:T(8,128)}), f32[1536,512]{1,0:T(8,128)}) %all-reduce.5.cloned.1.call-update) | async-done | bytes 3145744 | tf_op jit(solution)/shard_map/psum | solution.py:12
  545.1 9.6 %fusion.1 = f32[1536,512]{1,0:T(8,128)S(1)} fusion(f32[1536,512]{1,0:T(8,128)} %all-reduce.5.cloned.1.call-done, f32[512,512]{1,0:T(8,128)} %all-reduce.7.cloned.1.call-done, f32[1536]{0:T(1024)S(1)} %get-tuple-element.49, f32[512]{0:T(512)S(1)} %fusion.15, f32[1536]{0:T(1024)S(1)} %broadcast_in_dim.45, pred[1536]{0:T(1024)(128)(4,1)S(1)} %get-tuple-element.50, ...), kind=kOutput, calls=%fused_computation.7 | convolution fusion | flops 4835770368 | bytes 10501632 | tf_op jit(solution)/shard_map/dot_general | solution.py:20
  554.7 1.1 slice_select_fusion
  555.8 0.3 all-reduce.9.cloned.1.call-start
  556.1 7.5 convolution_select_fusion
  563.6 141.0 %all-reduce.11.cloned.1.call-done = f32[512,512]{1,0:T(8,128)} async-done(((f32[512,512]{1,0:T(8,128)}), f32[512,512]{1,0:T(8,128)}) %all-reduce.11.cloned.1.call-update) | async-done | bytes 1048592 | tf_op jit(solution)/shard_map/psum | solution.py:12
  704.6 142.5 %all-reduce.9.cloned.1.call-done = f32[1536,512]{1,0:T(8,128)} async-done(((f32[1536,512]{1,0:T(8,128)}), f32[1536,512]{1,0:T(8,128)}) %all-reduce.9.cloned.1.call-update) | async-done | bytes 3145744 | tf_op jit(solution)/shard_map/psum | solution.py:12
  847.1 9.9 %fusion.3 = f32[1536,512]{1,0:T(8,128)} fusion(f32[1536,512]{1,0:T(8,128)} %all-reduce.9.cloned.1.call-done, f32[1536,512]{1,0:T(8,128)S(1)} %fusion.1, f32[512,512]{1,0:T(8,128)} %all-reduce.11.cloned.1.call-done, f32[1536]{0:T(1024)S(1)} %get-tuple-element.52, f32[512]{0:T(512)S(1)} %fusion.16, f32[1536]{0:T(1024)S(1)} %broadcast_in_dim.45, ...), kind=kOutput, calls=%fused_computation.9 | convolution fusion | flops 4835770368 | bytes 10501632 | tf_op jit(solution)/shard_map/dot_general | solution.py:20
  (28 shorter events, 0.7 us)
Async XLA Ops:
  7.4 78.7 %collective-permute-start = (f32[64,12288]{1,0:T(8,128)}, f32[64,12288]{1,0:T(8,128)}, u32[]{:S(2)}, u32[]{:S(2)}) collective-permute-start(f32[64,12288]{1,0:T(8,128)} %bitcast.36), channel_id=1, source_target_pairs={{0,128},{128,0},{1,129},{129,1},{2,130},{130,2},{3,131},{131,3},{4... | collective-permute-start | bytes 9437192 | tf_op jit(solution)/shard_map/ppermute | solution.py:16
  11.1 5.9 copy-start
  17.0 4.0 copy-start.2
  162.7 8.4 copy-start.1
  162.7 90.9 %all-to-all-start = ((f32[64,8,1536]{2,0,1:T(8,128)}), f32[64,8,1536]{2,0,1:T(8,128)S(1)}, u32[]{:S(2)}, u32[]{:S(2)}) async-start(f32[64,8,1536]{2,0,1:T(8,128)} %copy.13), calls=%async_computation | async-start | bytes 6291456 | tf_op jit(solution)/shard_map/all_to_all | solution.py:44
  171.0 87.6 %all-gather.5.cloned.1.call-start = ((), (), s32[]{:S(2)}) async-start(), calls=%async_computation.5 | async-start | bytes 1179648 | tf_op jit(solution)/shard_map/all_gather | solution.py:62
  171.8 231.0 %all-reduce.7.cloned.1.call-start = ((), (), s32[]{:S(2)}) async-start(), calls=%async_computation.2 | async-start | bytes 2097152 | tf_op jit(solution)/shard_map/psum | solution.py:12
  258.3 286.8 %all-reduce.5.cloned.1.call-start = ((), (), s32[]{:S(2)}) async-start(), calls=%async_computation.1 | async-start | bytes 6291456 | tf_op jit(solution)/shard_map/psum | solution.py:12
  271.0 0.8 copy-start.3
  271.0 285.1 %all-gather.7.cloned.1.call-start = ((), (), s32[]{:S(2)}) async-start(), calls=%async_computation.6 | async-start | bytes 1179648 | tf_op jit(solution)/shard_map/all_gather | solution.py:62
  271.8 432.8 %all-reduce.11.cloned.1.call-start = ((), (), s32[]{:S(2)}) async-start(), calls=%async_computation.4 | async-start | bytes 2097152 | tf_op jit(solution)/shard_map/psum | solution.py:12
  555.8 291.3 %all-reduce.9.cloned.1.call-start = ((), (), s32[]{:S(2)}) async-start(), calls=%async_computation.3 | async-start | bytes 6291456 | tf_op jit(solution)/shard_map/psum | solution.py:12
Sparse Core Ops, SparseCore 0:
  173.7 55.4 all-gather.4
  273.6 30.5 all-gather.6
Sparse Core Ops, SparseCore 1:
  258.4 144.4 all-reduce.6
  405.6 139.5 all-reduce.4
  555.9 148.6 all-reduce.10
  707.3 139.7 all-reduce.8
where the time goes:
time: 865 us
  waiting for transfers between devices  639 us (74%)
  other arithmetic  133 us (15%)
  matrix products  39.3 us (5%)
  local copies, waits for them, and re-layouts  24.9 us (3%)
  between operations  15.2 us (2%)
  starting transfers between devices  12.7 us (1%)
    psum x4, waiting for transfers between devices, broadcast(): return lax.psum(kept, axis)  557 us
    scatter-add x2, other arithmetic, extend_add(): return target.at[:, target_rows].add(child_rows, mode='drop')  129 us
    all_to_all x1, waiting for transfers between devices, local(): lax.all_to_all(assembled, 'row', split_axis=1, concat_axis=0, tiled=True)  81.7 us
    dot_general x4, matrix products, product(): jnp.dot(left, right, precision=lax.Precision.HIGHEST, preferred_element_t...  39.3 us
  transfers between devices with their start and end apart: 8, of which 5 were waited for; matrix products, arithmetic and copies ran while one was open for 13% of the time, Pallas kernels for 0%

commit v1 on v0

--- a/solution.py
+++ b/solution.py
@@ -9,7 +9,7 @@
 
 def broadcast(value, axis, source):
     kept = jnp.where(lax.axis_index(axis) == source, value, 0).astype(value.dtype)
-    return lax.psum(kept, axis)
+    return jnp.sum(lax.all_gather(kept, axis_name=axis), axis=0)
 
 
 def from_partner(x, axis, distance):

time: 865 us -> 1280 us (1.48)
  waiting for transfers between devices: 639 us -> 1000 us
  other arithmetic: 133 us -> 191 us
    all_gather x0 -> x4, waiting for transfers between devices: none -> 915 us  [broadcast(): return jnp.sum(lax.all_gather(kept, axis_name=axis), axis=0)]
    psum x4 -> x0, waiting for transfers between devices: 557 us -> none  [broadcast(): return lax.psum(kept, axis)]
    reduce_sum x0 -> x4, other arithmetic: none -> 58.2 us  [broadcast(): return jnp.sum(lax.all_gather(kept, axis_name=axis), axis=0)]
  transfers between devices with their start and end apart: 8 -> 8, of which waited for: 5 -> 6; matrix products, arithmetic and copies ran while one was open for 13% -> 12% of each run, Pallas kernels for 0% -> 0%
where the time goes in v1:
time: 1280 us
  waiting for transfers between devices  1000 us (78%)
  other arithmetic  191 us (15%)
  matrix products  39.1 us (3%)
  local copies, waits for them, and re-layouts  25 us (2%)
  between operations  13.6 us (1%)
    all_gather x4, waiting for transfers between devices, broadcast(): return jnp.sum(lax.all_gather(kept, axis_name=axis), axis=0)  915 us
    scatter-add x2, other arithmetic, extend_add(): return target.at[:, target_rows].add(child_rows, mode='drop')  129 us
    all_to_all x1, waiting for transfers between devices, local(): lax.all_to_all(assembled, 'row', split_axis=1, concat_axis=0, tiled=True)  81.7 us
    reduce_sum x4, other arithmetic, broadcast(): return jnp.sum(lax.all_gather(kept, axis_name=axis), axis=0)  58.2 us
    dot_general x4, matrix products, product(): jnp.dot(left, right, precision=lax.Precision.HIGHEST, preferred_element_t...  39.1 us
  transfers between devices with their start and end apart: 8, of which 6 were waited for; matrix products, arithmetic and copies ran while one was open for 12% of the time, Pallas kernels for 0%

profile of v1, /device:TPU:1, one launch (start us, length us, event | category | flops | bytes accessed | tf_op | source)
XLA Modules:
  0.0 1283.8 jit_solution(13825796733814715265)
XLA Ops:
  6.5 3.7 collective-permute-start
  10.3 5.9 copy.10
  16.2 4.0 copy.11
  20.5 64.7 %scatter_fusion = f32[64,12288]{0,1:T(8,128)} fusion(f32[64,12288]{0,1:T(8,128)} %bitcast.35, s32[12288]{0:T(1024)S(1)} %bitcast.47, f32[12288,64]{1,0:T(8,128)} %copy.11), kind=kCustom, calls=%fused_computation | custom fusion | flops 786432 | bytes 9486336 | tf_op jit(solution)/shard_map/scatter-add | solution.py:27
  85.2 5.8 copy.12
  91.0 64.7 %scatter_fusion.1 = f32[64,12288]{0,1:T(8,128)} fusion(f32[64,12288]{0,1:T(8,128)} %scatter_fusion, s32[12288]{0:T(1024)S(1)} %bitcast.46, f32[12288,64]{1,0:T(8,128)} %copy.12), kind=kCustom, calls=%fused_computation.1 | custom fusion | flops 786432 | bytes 9486336 | tf_op jit(solution)/shard_map/scatter-add | solution.py:27
  155.7 6.1 copy.13
  161.8 8.3 all-to-all-start
  171.0 81.7 %all-to-all-done = f32[64,8,1536]{2,0,1:T(8,128)S(1)} async-done(((f32[64,8,1536]{2,0,1:T(8,128)}), f32[64,8,1536]{2,0,1:T(8,128)S(1)}, u32[]{:S(2)}, u32[]{:S(2)}) %all-to-all-start) | async-done | bytes 3145760 | tf_op jit(solution)/shard_map/all_to_all | solution.py:44
  252.7 2.4 copy.14
  255.1 2.3 slice_select_fusion.1
  257.7 12.4 convolution_select_fusion.1
  270.9 206.9 %all-gather.17.cloned.1.call-done = f32[8192,512]{1,0:T(8,128)} async-done(((f32[512,512]{1,0:T(8,128)}), f32[8192,512]{1,0:T(8,128)}) %all-gather.17.cloned.1.call-update) | async-done | bytes 16777232 | tf_op jit(solution)/shard_map/all_gather | solution.py:12
  477.7 8.9 reduce_sum.37
  486.6 242.8 %all-gather.15.cloned.1.call-done = f32[24576,512]{1,0:T(8,128)} async-done(((f32[1536,512]{1,0:T(8,128)}), f32[24576,512]{1,0:T(8,128)}) %all-gather.15.cloned.1.call-update) | async-done | bytes 50331664 | tf_op jit(solution)/shard_map/all_gather | solution.py:12
  729.4 20.2 %reduce_sum.36 = f32[1536,512]{1,0:T(8,128)} reduce(f32[16,1536,512]{2,1,0:T(8,128)} %bitcast.37, f32[]{:T(128)} %constant.114.clone.1), dimensions={0}, to_apply=%region_2.3 | reduce | flops 11796480 | bytes 53477380 | tf_op jit(solution)/shard_map/reduce_sum | solution.py:12
  749.7 9.6 fusion.1
  760.6 4.4 all-gather.19.cloned.1.call-done
  765.0 7.4 convolution_select_fusion
  772.5 223.0 %all-gather.23.cloned.1.call-done = f32[8192,512]{1,0:T(8,128)} async-done(((f32[512,512]{1,0:T(8,128)}), f32[8192,512]{1,0:T(8,128)}) %all-gather.23.cloned.1.call-update) | async-done | bytes 16777232 | tf_op jit(solution)/shard_map/all_gather | solution.py:12
  995.5 8.9 reduce_sum.39
  1004.4 242.7 %all-gather.21.cloned.1.call-done = f32[24576,512]{1,0:T(8,128)} async-done(((f32[1536,512]{1,0:T(8,128)}), f32[24576,512]{1,0:T(8,128)}) %all-gather.21.cloned.1.call-update) | async-done | bytes 50331664 | tf_op jit(solution)/shard_map/all_gather | solution.py:12
  1247.0 20.2 %reduce_sum.38 = f32[1536,512]{1,0:T(8,128)} reduce(f32[16,1536,512]{2,1,0:T(8,128)} %bitcast.38, f32[]{:T(128)} %constant.114.clone.1), dimensions={0}, to_apply=%region_4.5 | reduce | flops 11796480 | bytes 53477380 | tf_op jit(solution)/shard_map/reduce_sum | solution.py:12
  1267.3 9.7 fusion.3
  (32 shorter events, 3.4 us)
Async XLA Ops:
  6.5 78.7 %collective-permute-start = (f32[64,12288]{1,0:T(8,128)}, f32[64,12288]{1,0:T(8,128)}, u32[]{:S(2)}, u32[]{:S(2)}) collective-permute-start(f32[64,12288]{1,0:T(8,128)} %bitcast.44), channel_id=1, source_target_pairs={{0,128},{128,0},{1,129},{129,1},{2,130},{130,2},{3,131},{131,3},{4... | collective-permute-start | bytes 9437192 | tf_op jit(solution)/shard_map/ppermute | solution.py:16
  10.3 5.9 copy-start
  16.2 4.0 copy-start.2
  161.8 8.4 copy-start.1
  161.8 90.9 %all-to-all-start = ((f32[64,8,1536]{2,0,1:T(8,128)}), f32[64,8,1536]{2,0,1:T(8,128)S(1)}, u32[]{:S(2)}, u32[]{:S(2)}) async-start(f32[64,8,1536]{2,0,1:T(8,128)} %copy.13), calls=%async_computation | async-start | bytes 6291456 | tf_op jit(solution)/shard_map/all_to_all | solution.py:44
  170.1 87.5 %all-gather.13.cloned.1.call-start = ((), (), s32[]{:S(2)}) async-start(), calls=%async_computation.1 | async-start | bytes 1179648 | tf_op jit(solution)/shard_map/all_gather | solution.py:62
  170.9 306.8 %all-gather.17.cloned.1.call-start = ((), (), s32[]{:S(2)}) async-start(), calls=%async_computation.3 | async-start | bytes 17825792 | tf_op jit(solution)/shard_map/all_gather | solution.py:12
  257.4 472.0 %all-gather.15.cloned.1.call-start = ((), (), s32[]{:S(2)}) async-start(), calls=%async_computation.2 | async-start | bytes 53477376 | tf_op jit(solution)/shard_map/all_gather | solution.py:12
  270.1 0.7 copy-start.3
  270.1 494.9 %all-gather.19.cloned.1.call-start = ((), (), s32[]{:S(2)}) async-start(), calls=%async_computation.4 | async-start | bytes 1179648 | tf_op jit(solution)/shard_map/all_gather | solution.py:62
  270.7 724.8 %all-gather.23.cloned.1.call-start = ((), (), s32[]{:S(2)}) async-start(), calls=%async_computation.6 | async-start | bytes 17825792 | tf_op jit(solution)/shard_map/all_gather | solution.py:12
  760.4 486.7 %all-gather.21.cloned.1.call-start = ((), (), s32[]{:S(2)}) async-start(), calls=%async_computation.5 | async-start | bytes 53477376 | tf_op jit(solution)/shard_map/all_gather | solution.py:12
Sparse Core Ops, SparseCore 0:
  172.8 55.7 all-gather.12
  257.5 220.1 all-gather.16
  479.6 249.7 all-gather.14
  731.1 33.9 all-gather.18
  767.4 228.0 all-gather.22
  997.2 249.7 all-gather.20

commit v2 on v0

--- a/solution.py
+++ b/solution.py
@@ -41,7 +41,10 @@
     assembled = front_entries[0, 0]
     assembled = extend_add(assembled, own_block, own_map, subcube_side * half_rows)
     assembled = extend_add(assembled, partner_block, partner_map, subcube_side * half_rows)
-    regrouped = lax.all_to_all(assembled, "row", split_axis=1, concat_axis=0, tiled=True)
+    size = lax.axis_size("row")
+    tiles = jnp.stack(jnp.split(assembled, size, axis=1), axis=0)
+    tiles = lax.all_to_all(tiles, "row", split_axis=0, concat_axis=0)
+    regrouped = jnp.concatenate(tiles, axis=0)
     local_block = regrouped.T
     row_count = local_block.shape[0]
     block_width = local_block.shape[1]

time: 865 us -> 882 us (1.020)
  local copies, waits for them, and re-layouts: 24.9 us -> 41.5 us
    unnamed x9 -> x16, local copies, waits for them, and re-layouts: 5.92 us -> 20.4 us
where the time goes in v2:
time: 882 us; the launch traced here: 881 us
  waiting for transfers between devices  639 us (72%)
  other arithmetic  133 us (15%)
  local copies, waits for them, and re-layouts  41.5 us (5%)
  matrix products  39.3 us (4%)
  between operations  15.2 us (2%)
  starting transfers between devices  12.7 us (1%)
    psum x4, waiting for transfers between devices, broadcast(): return lax.psum(kept, axis)  557 us
    scatter-add x2, other arithmetic, extend_add(): return target.at[:, target_rows].add(child_rows, mode='drop')  129 us
    all_to_all x1, waiting for transfers between devices, local(): tiles = lax.all_to_all(tiles, 'row', split_axis=0, concat_axis=0)  81.7 us
    dot_general x4, matrix products, product(): jnp.dot(left, right, precision=lax.Precision.HIGHEST, preferred_element_t...  39.3 us
    unnamed x16, local copies, waits for them, and re-layouts  20.4 us
  transfers between devices with their start and end apart: 8, of which 5 were waited for; matrix products, arithmetic and copies ran while one was open for 13% of the time, Pallas kernels for 0%

profile of v2, /device:TPU:1, one launch (start us, length us, event | category | flops | bytes accessed | tf_op | source)
XLA Modules:
  0.0 881.1 jit_solution(17679707837251174198)
XLA Ops:
  7.4 3.7 collective-permute-start
  11.1 5.9 copy.15
  17.0 4.0 copy.16
  21.3 64.7 %scatter_fusion = f32[64,12288]{0,1:T(8,128)} fusion(f32[64,12288]{0,1:T(8,128)} %bitcast.60, s32[12288]{0:T(1024)S(1)} %bitcast.67, f32[12288,64]{1,0:T(8,128)} %copy.16), kind=kCustom, calls=%fused_computation | custom fusion | flops 786432 | bytes 9486336 | tf_op jit(solution)/shard_map/scatter-add | solution.py:27
  86.1 5.8 copy.17
  91.8 64.7 %scatter_fusion.1 = f32[64,12288]{0,1:T(8,128)} fusion(f32[64,12288]{0,1:T(8,128)} %scatter_fusion, s32[12288]{0:T(1024)S(1)} %bitcast.66, f32[12288,64]{1,0:T(8,128)} %copy.17), kind=kCustom, calls=%fused_computation.1 | custom fusion | flops 786432 | bytes 9486336 | tf_op jit(solution)/shard_map/scatter-add | solution.py:27
  156.6 2.1 fusion.13
  158.6 2.1 fusion.12
  164.8 2.1 fusion.9
  169.0 2.1 fusion.7
  171.1 2.1 fusion.6
  173.1 6.1 copy.18
  179.3 8.3 all-to-all-start
  188.4 81.7 %all-to-all-done = f32[8,64,1536]{2,1,0:T(8,128)S(1)} async-done(((f32[8,64,1536]{2,1,0:T(8,128)}), f32[8,64,1536]{2,1,0:T(8,128)S(1)}, u32[]{:S(2)}, u32[]{:S(2)}) %all-to-all-start) | async-done | bytes 3145760 | tf_op jit(solution)/shard_map/all_to_all | solution.py:46
  270.2 2.3 copy.19
  272.5 2.4 slice_select_fusion.1
  275.2 12.4 %convolution_select_fusion.1 = f32[1536,512]{1,0:T(8,128)} fusion(f32[512,1536]{1,0:T(8,128)S(1)} %bitcast.62, pred[]{:T(512)S(6)} %eq.13, f32[1,512,512]{2,1,0:T(8,128)} %all-gather.5.cloned.1.call-done), kind=kOutput, calls=%fused_computation.3 | convolution fusion | flops 4832624640 | bytes 7340033 | tf_op jit(solution)/shard_map/dot_general | solution.py:20
  288.5 130.9 %all-reduce.7.cloned.1.call-done = f32[512,512]{1,0:T(8,128)} async-done(((f32[512,512]{1,0:T(8,128)}), f32[512,512]{1,0:T(8,128)}) %all-reduce.7.cloned.1.call-update) | async-done | bytes 1048592 | tf_op jit(solution)/shard_map/psum | solution.py:12
  419.4 142.3 %all-reduce.5.cloned.1.call-done = f32[1536,512]{1,0:T(8,128)} async-done(((f32[1536,512]{1,0:T(8,128)}), f32[1536,512]{1,0:T(8,128)}) %all-reduce.5.cloned.1.call-update) | async-done | bytes 3145744 | tf_op jit(solution)/shard_map/psum | solution.py:12
  561.7 9.6 %fusion.1 = f32[1536,512]{1,0:T(8,128)S(1)} fusion(f32[1536,512]{1,0:T(8,128)} %all-reduce.5.cloned.1.call-done, f32[512,512]{1,0:T(8,128)} %all-reduce.7.cloned.1.call-done, f32[1536]{0:T(1024)S(1)} %get-tuple-element.49, f32[512]{0:T(512)S(1)} %fusion.23, f32[1536]{0:T(1024)S(1)} %broadcast_in_dim.45, pred[1536]{0:T(1024)(128)(4,1)S(1)} %get-tuple-element.50, ...), kind=kOutput, calls=%fused_computation.7 | convolution fusion | flops 4835770368 | bytes 10501632 | tf_op jit(solution)/shard_map/dot_general | solution.py:20
  572.7 7.5 convolution_select_fusion
  580.2 141.0 %all-reduce.11.cloned.1.call-done = f32[512,512]{1,0:T(8,128)} async-done(((f32[512,512]{1,0:T(8,128)}), f32[512,512]{1,0:T(8,128)}) %all-reduce.11.cloned.1.call-update) | async-done | bytes 1048592 | tf_op jit(solution)/shard_map/psum | solution.py:12
  721.2 142.5 %all-reduce.9.cloned.1.call-done = f32[1536,512]{1,0:T(8,128)} async-done(((f32[1536,512]{1,0:T(8,128)}), f32[1536,512]{1,0:T(8,128)}) %all-reduce.9.cloned.1.call-update) | async-done | bytes 3145744 | tf_op jit(solution)/shard_map/psum | solution.py:12
  863.6 9.9 %fusion.3 = f32[1536,512]{1,0:T(8,128)} fusion(f32[1536,512]{1,0:T(8,128)} %all-reduce.9.cloned.1.call-done, f32[1536,512]{1,0:T(8,128)S(1)} %fusion.1, f32[512,512]{1,0:T(8,128)} %all-reduce.11.cloned.1.call-done, f32[1536]{0:T(1024)S(1)} %get-tuple-element.52, f32[512]{0:T(512)S(1)} %fusion.24, f32[1536]{0:T(1024)S(1)} %broadcast_in_dim.45, ...), kind=kOutput, calls=%fused_computation.9 | convolution fusion | flops 4835770368 | bytes 10501632 | tf_op jit(solution)/shard_map/dot_general | solution.py:20
  (36 shorter events, 9.8 us)
Async XLA Ops:
  7.4 78.7 %collective-permute-start = (f32[64,12288]{1,0:T(8,128)}, f32[64,12288]{1,0:T(8,128)}, u32[]{:S(2)}, u32[]{:S(2)}) collective-permute-start(f32[64,12288]{1,0:T(8,128)} %bitcast.64), channel_id=1, source_target_pairs={{0,128},{128,0},{1,129},{129,1},{2,130},{130,2},{3,131},{131,3},{4... | collective-permute-start | bytes 9437192 | tf_op jit(solution)/shard_map/ppermute | solution.py:16
  11.1 5.9 copy-start
  17.0 4.0 copy-start.2
  179.3 8.4 copy-start.1
  179.3 90.9 %all-to-all-start = ((f32[8,64,1536]{2,1,0:T(8,128)}), f32[8,64,1536]{2,1,0:T(8,128)S(1)}, u32[]{:S(2)}, u32[]{:S(2)}) async-start(f32[8,64,1536]{2,1,0:T(8,128)} %copy.18), calls=%async_computation | async-start | bytes 6291456 | tf_op jit(solution)/shard_map/all_to_all | solution.py:46
  187.6 87.6 %all-gather.5.cloned.1.call-start = ((), (), s32[]{:S(2)}) async-start(), calls=%async_computation.5 | async-start | bytes 1179648 | tf_op jit(solution)/shard_map/all_gather | solution.py:65
  188.4 231.0 %all-reduce.7.cloned.1.call-start = ((), (), s32[]{:S(2)}) async-start(), calls=%async_computation.2 | async-start | bytes 2097152 | tf_op jit(solution)/shard_map/psum | solution.py:12
  274.9 286.8 %all-reduce.5.cloned.1.call-start = ((), (), s32[]{:S(2)}) async-start(), calls=%async_computation.1 | async-start | bytes 6291456 | tf_op jit(solution)/shard_map/psum | solution.py:12
  287.6 0.8 copy-start.3
  287.6 285.1 %all-gather.7.cloned.1.call-start = ((), (), s32[]{:S(2)}) async-start(), calls=%async_computation.6 | async-start | bytes 1179648 | tf_op jit(solution)/shard_map/all_gather | solution.py:65
  288.3 432.8 %all-reduce.11.cloned.1.call-start = ((), (), s32[]{:S(2)}) async-start(), calls=%async_computation.4 | async-start | bytes 2097152 | tf_op jit(solution)/shard_map/psum | solution.py:12
  572.4 291.3 %all-reduce.9.cloned.1.call-start = ((), (), s32[]{:S(2)}) async-start(), calls=%async_computation.3 | async-start | bytes 6291456 | tf_op jit(solution)/shard_map/psum | solution.py:12
Sparse Core Ops, SparseCore 0:
  190.3 55.4 all-gather.4
  290.2 30.5 all-gather.6
Sparse Core Ops, SparseCore 1:
  275.0 144.4 all-reduce.6
  422.1 139.5 all-reduce.4
  572.5 148.6 all-reduce.10
  723.9 139.7 all-reduce.8
